TPU v7x, 128 devices: a whole 4x4x4 slice. The times are simulated.
128 devices in a mesh: month: 8 (over y, core), cols: 16 (over x, z).
Axes of the slice: x: 4, y: 4, z: 4, core: 2. Of those that a mesh axis runs over, the one named last changes fastest.
Arguments:
- forcing: float32 [8, 256, 6, 128], P('month', 'cols'), may hold values from -6 to 6
- tiles: bfloat16 [8, 4096, 128, 128], P('month', 'cols'), may hold values from -0.21875 to 0.21875
- tile_rows: int32 [8, 4096], P('month', 'cols'), may hold values from 0 to 255, as said below
- tile_cols: int32 [8, 4096], P('month', 'cols'), may hold values from 0 to 255, as said below
- tile_count: int32 [8, 16], P('month', 'cols'), may hold values from 1 to 256, as said below
- depth: int32 [256, 16], P('cols'), may hold values from 1 to 8
Outputs:
- adjoint: float32 [8, 256, 6, 128], P('month', 'cols')
Inputs may be any that keep to these rules, and one draw needn't show every extreme that they name: `tile_cols`: the tiles held by cols index c take their column blocks from c's own blocks, c * 16 to (c + 1) * 16 - 1. `tile_rows`: the tiles held by cols index c take their row blocks from the blocks of c, of its two neighbours c - 1 and c + 1, and of the index c + 8, all counted modulo 256 / 16. `tile_count`: in each month one cols index has all 256 slots live; slots from the count on are unused.
All inputs are finite; a program needn't handle non-finite values.
Results may differ from a plain program's by a relative error of at most 0.022.
Values may be sent and summed in bfloat16 or wider, within the bound.
A program may use at most 64 MiB of HBM per device.

v0:
```python
import jax
import jax.numpy as jnp
from jax import lax
from jax.sharding import PartitionSpec as P


def from_behind(shard, axis, by):
    length = lax.axis_size(axis)
    return lax.ppermute(shard, axis, [(i, (i + by) % length) for i in range(length)])


def wet_mask(depth, block):
    width = depth.shape[1]
    level = jnp.arange(block, dtype=jnp.int32) // width
    spread = jnp.tile(depth, (1, block // width))
    return (level[None, :] < spread).astype(jnp.float32)[:, None, :]


def place(buffer, terms, target, inside):
    return buffer.at[target].add(terms * inside.astype(jnp.float32)[:, None, None])


def terms_for(x_vals, active, plates, rows_all, local_cols, count, target_fn, span):
    slots = plates.shape[0]
    tracers = x_vals.shape[1]
    block = x_vals.shape[2]
    empty = jnp.zeros((span, tracers, block), jnp.float32)

    def compute(unused):
        picked = x_vals[local_cols]
        terms = jnp.einsum("stj,sij->sti", picked, plates, preferred_element_type=jnp.float32)
        valid = jnp.arange(slots, dtype=jnp.int32) < count
        target, inside = target_fn(rows_all)
        return place(empty, terms, target, inside & valid)

    return lax.cond(active, compute, lambda unused: empty, 0)


def on_device(forcing, tiles, tile_rows, tile_cols, tile_count, depth):
    months = lax.axis_size("month")
    my_month = lax.axis_index("month")
    ncols = lax.axis_size("cols")
    my_cols = lax.axis_index("cols")
    blk_local, tracers, block = forcing.shape[1:]
    nblk = blk_local * ncols
    wet = wet_mask(depth, block)

    def reduce_terms(x_vals, active, plates, rows_all, local_cols, count):

        def target_fn(rows):
            return (rows, rows >= 0)

        partial_terms = terms_for(
            x_vals, active, plates, rows_all, local_cols, count, target_fn, nblk
        )
        return lax.psum_scatter(
            partial_terms.astype(jnp.bfloat16), "cols", scatter_dimension=0, tiled=True
        ).astype(jnp.float32)

    def turn(step, carry):
        received, result = carry
        month_now = months - 1 - step % months
        active = my_month == month_now
        plates = tiles[0]
        rows_all = tile_rows[0]
        cols_here = tile_cols[0]
        count = tile_count[0, 0]
        own = forcing[0]
        local_cols = cols_here - my_cols * blk_local
        x_vals = (received + own).astype(jnp.bfloat16)
        summed = reduce_terms(x_vals, active, plates, rows_all, local_cols, count)
        state = wet * summed
        result = jnp.where((my_month == month_now) & (step >= months), state, result)
        sending = jnp.where(active, state, jnp.zeros_like(state))
        received = from_behind(sending.astype(jnp.bfloat16), "month", -1).astype(sending.dtype)
        return (received, result)

    start_state = jnp.zeros((blk_local, tracers, block), jnp.float32)
    final_carry, result = lax.fori_loop(0, 2 * months, turn, (start_state, start_state))
    return result[None]


def solution(mesh):
    in_specs = (
        P("month", "cols", None, None),
        P("month", "cols", None, None),
        P("month", "cols"),
        P("month", "cols"),
        P("month", "cols"),
        P("cols", None),
    )
    out_specs = P("month", "cols", None, None)
    return jax.shard_map(
        on_device, mesh=mesh, in_specs=in_specs, out_specs=out_specs, check_vma=False
    )
```

profile of v0, /device:TPU:0, one launch (start us, length us, event | category | flops | bytes accessed | tf_op | source)
XLA Modules:
  0.0 1809.0 jit_solution(3437524578139409700)
XLA Ops:
  7.4 1794.4 %while.18 = (s32[]{:T(128)}, f32[16,6,128]{2,1,0:T(8,128)S(1)}, f32[16,6,128]{2,1,0:T(8,128)S(1)}, s32[]{:T(128)}, f32[1,16,6,128]{3,2,1,0:T(8,128)S(1)}, /*inde...) while((s32[]{:T(128)}, f32[16,6,128]{2,1,0:T(8,128)S(1)}, ...), condition=%wide.region_5.6_spmd.clone, body=%wide.region_0.5_spmd.clone.sunk | while | flops 51052300 | bytes 16585138 | solution.py:79
  7.5 1.1 conditional.3
  8.6 2.1 convert_element_type.103
  10.8 109.3 %reduce-scatter.2.cloned.1.call-done = bf16[16,6,128]{2,1,0:T(8,128)(2,1)} async-done(((bf16[256,6,128]{2,1,0:T(8,128)(2,1)}), bf16[16,6,128]{2,1,0:T(8,128)(2,1)}) %reduce-scatter.2.cloned.1.call-update) | async-done | bytes 24592 | tf_op jit(solution)/shard_map/while/body/eval_jaxpr/reduce_scatter | solution.py:56
  121.4 1.6 collective-permute-done
  123.1 1.1 conditional.3
  124.2 2.1 convert_element_type.103
  126.4 106.0 %reduce-scatter.2.cloned.1.call-done = bf16[16,6,128]{2,1,0:T(8,128)(2,1)} async-done(((bf16[256,6,128]{2,1,0:T(8,128)(2,1)}), bf16[16,6,128]{2,1,0:T(8,128)(2,1)}) %reduce-scatter.2.cloned.1.call-update) | async-done | bytes 24592 | tf_op jit(solution)/shard_map/while/body/eval_jaxpr/reduce_scatter | solution.py:56
  233.8 1.6 collective-permute-done
  235.5 1.1 conditional.3
  236.5 2.1 convert_element_type.103
  238.8 107.2 %reduce-scatter.2.cloned.1.call-done = bf16[16,6,128]{2,1,0:T(8,128)(2,1)} async-done(((bf16[256,6,128]{2,1,0:T(8,128)(2,1)}), bf16[16,6,128]{2,1,0:T(8,128)(2,1)}) %reduce-scatter.2.cloned.1.call-update) | async-done | bytes 24592 | tf_op jit(solution)/shard_map/while/body/eval_jaxpr/reduce_scatter | solution.py:56
  347.3 1.6 collective-permute-done
  349.0 1.1 conditional.3
  350.1 2.1 convert_element_type.103
  352.3 106.2 %reduce-scatter.2.cloned.1.call-done = bf16[16,6,128]{2,1,0:T(8,128)(2,1)} async-done(((bf16[256,6,128]{2,1,0:T(8,128)(2,1)}), bf16[16,6,128]{2,1,0:T(8,128)(2,1)}) %reduce-scatter.2.cloned.1.call-update) | async-done | bytes 24592 | tf_op jit(solution)/shard_map/while/body/eval_jaxpr/reduce_scatter | solution.py:56
  459.9 1.6 collective-permute-done
  461.6 1.1 conditional.3
  462.6 2.1 convert_element_type.103
  464.9 105.7 %reduce-scatter.2.cloned.1.call-done = bf16[16,6,128]{2,1,0:T(8,128)(2,1)} async-done(((bf16[256,6,128]{2,1,0:T(8,128)(2,1)}), bf16[16,6,128]{2,1,0:T(8,128)(2,1)}) %reduce-scatter.2.cloned.1.call-update) | async-done | bytes 24592 | tf_op jit(solution)/shard_map/while/body/eval_jaxpr/reduce_scatter | solution.py:56
  572.0 1.6 collective-permute-done
  574.7 2.1 convert_element_type.103
  577.0 104.6 %reduce-scatter.2.cloned.1.call-done = bf16[16,6,128]{2,1,0:T(8,128)(2,1)} async-done(((bf16[256,6,128]{2,1,0:T(8,128)(2,1)}), bf16[16,6,128]{2,1,0:T(8,128)(2,1)}) %reduce-scatter.2.cloned.1.call-update) | async-done | bytes 24592 | tf_op jit(solution)/shard_map/while/body/eval_jaxpr/reduce_scatter | solution.py:56
  682.9 1.6 collective-permute-done
  684.5 1.1 conditional.3
  685.6 2.1 convert_element_type.103
  687.8 104.9 %reduce-scatter.2.cloned.1.call-done = bf16[16,6,128]{2,1,0:T(8,128)(2,1)} async-done(((bf16[256,6,128]{2,1,0:T(8,128)(2,1)}), bf16[16,6,128]{2,1,0:T(8,128)(2,1)}) %reduce-scatter.2.cloned.1.call-update) | async-done | bytes 24592 | tf_op jit(solution)/shard_map/while/body/eval_jaxpr/reduce_scatter | solution.py:56
  794.1 1.6 collective-permute-done
  795.8 36.1 %conditional.3 = (f32[256,6,128]{2,1,0:T(8,128)}) conditional(s32[]{:T(128)} %convert_element_type.102, () %tuple.56, (s32[1,256]{1,0:T(1,128)}, s32[]{:T(128)}, s32[1,256]{1,0:T(1,128)}, bf16[16,6,128]{2,1,0:T(8,128)(2,1)S(1)}, bf16[1,256,128,128]{3,2,1,0:T(8,128)(2,1)}, /*index=5*/s32[1,1]{1,0:T(1,128)}) %tuple.57), branch_computations={%region_1.1_spmd, %region_2.3_spmd} | conditional | flops 50728704 | bytes 13515284 | solution.py:36
  798.7 6.7 fusion.4
  806.5 25.4 %scatter_fusion = f32[256,6,128]{2,1,0:T(8,128)} fusion(f32[256,6,128]{2,1,0:T(8,128)} %broadcast.103, s32[256]{0:T(256)S(1)} %bitcast.26, f32[256,6,128]{2,1,0:T(8,128)S(1)} %fusion.4), kind=kCustom, calls=%fused_computation.1 | custom fusion | flops 196608 | bytes 2360320 | tf_op jit(solution)/shard_map/while/body/eval_jaxpr/cond/branch_1_fun/scatter-add | solution.py:20
  831.9 2.1 convert_element_type.103
  834.2 69.0 %reduce-scatter.2.cloned.1.call-done = bf16[16,6,128]{2,1,0:T(8,128)(2,1)} async-done(((bf16[256,6,128]{2,1,0:T(8,128)(2,1)}), bf16[16,6,128]{2,1,0:T(8,128)(2,1)}) %reduce-scatter.2.cloned.1.call-update) | async-done | bytes 24592 | tf_op jit(solution)/shard_map/while/body/eval_jaxpr/reduce_scatter | solution.py:56
  904.6 1.6 collective-permute-done
  906.2 1.1 conditional.3
  907.3 2.1 convert_element_type.103
  909.5 106.5 %reduce-scatter.2.cloned.1.call-done = bf16[16,6,128]{2,1,0:T(8,128)(2,1)} async-done(((bf16[256,6,128]{2,1,0:T(8,128)(2,1)}), bf16[16,6,128]{2,1,0:T(8,128)(2,1)}) %reduce-scatter.2.cloned.1.call-update) | async-done | bytes 24592 | tf_op jit(solution)/shard_map/while/body/eval_jaxpr/reduce_scatter | solution.py:56
  1017.4 1.6 collective-permute-done
  1020.1 2.1 convert_element_type.103
  1022.3 105.9 %reduce-scatter.2.cloned.1.call-done = bf16[16,6,128]{2,1,0:T(8,128)(2,1)} async-done(((bf16[256,6,128]{2,1,0:T(8,128)(2,1)}), bf16[16,6,128]{2,1,0:T(8,128)(2,1)}) %reduce-scatter.2.cloned.1.call-update) | async-done | bytes 24592 | tf_op jit(solution)/shard_map/while/body/eval_jaxpr/reduce_scatter | solution.py:56
  1129.7 1.6 collective-permute-done
  1131.3 1.1 conditional.3
  1132.4 2.1 convert_element_type.103
  1134.6 107.1 %reduce-scatter.2.cloned.1.call-done = bf16[16,6,128]{2,1,0:T(8,128)(2,1)} async-done(((bf16[256,6,128]{2,1,0:T(8,128)(2,1)}), bf16[16,6,128]{2,1,0:T(8,128)(2,1)}) %reduce-scatter.2.cloned.1.call-update) | async-done | bytes 24592 | tf_op jit(solution)/shard_map/while/body/eval_jaxpr/reduce_scatter | solution.py:56
  1243.1 1.6 collective-permute-done
  1244.8 1.1 conditional.3
  1245.9 2.1 convert_element_type.103
  1248.1 106.2 %reduce-scatter.2.cloned.1.call-done = bf16[16,6,128]{2,1,0:T(8,128)(2,1)} async-done(((bf16[256,6,128]{2,1,0:T(8,128)(2,1)}), bf16[16,6,128]{2,1,0:T(8,128)(2,1)}) %reduce-scatter.2.cloned.1.call-update) | async-done | bytes 24592 | tf_op jit(solution)/shard_map/while/body/eval_jaxpr/reduce_scatter | solution.py:56
  1355.7 1.6 collective-permute-done
  1358.4 2.1 convert_element_type.103
  1360.6 105.7 %reduce-scatter.2.cloned.1.call-done = bf16[16,6,128]{2,1,0:T(8,128)(2,1)} async-done(((bf16[256,6,128]{2,1,0:T(8,128)(2,1)}), bf16[16,6,128]{2,1,0:T(8,128)(2,1)}) %reduce-scatter.2.cloned.1.call-update) | async-done | bytes 24592 | tf_op jit(solution)/shard_map/while/body/eval_jaxpr/reduce_scatter | solution.py:56
  1467.7 1.6 collective-permute-done
  1470.5 2.1 convert_element_type.103
  1472.7 104.5 %reduce-scatter.2.cloned.1.call-done = bf16[16,6,128]{2,1,0:T(8,128)(2,1)} async-done(((bf16[256,6,128]{2,1,0:T(8,128)(2,1)}), bf16[16,6,128]{2,1,0:T(8,128)(2,1)}) %reduce-scatter.2.cloned.1.call-update) | async-done | bytes 24592 | tf_op jit(solution)/shard_map/while/body/eval_jaxpr/reduce_scatter | solution.py:56
  1578.6 1.6 collective-permute-done
  1581.3 2.1 convert_element_type.103
  1583.5 104.9 %reduce-scatter.2.cloned.1.call-done = bf16[16,6,128]{2,1,0:T(8,128)(2,1)} async-done(((bf16[256,6,128]{2,1,0:T(8,128)(2,1)}), bf16[16,6,128]{2,1,0:T(8,128)(2,1)}) %reduce-scatter.2.cloned.1.call-update) | async-done | bytes 24592 | tf_op jit(solution)/shard_map/while/body/eval_jaxpr/reduce_scatter | solution.py:56
  1689.8 1.6 collective-permute-done
  1691.5 36.1 %conditional.3 = (f32[256,6,128]{2,1,0:T(8,128)}) conditional(s32[]{:T(128)} %convert_element_type.102, () %tuple.56, (s32[1,256]{1,0:T(1,128)}, s32[]{:T(128)}, s32[1,256]{1,0:T(1,128)}, bf16[16,6,128]{2,1,0:T(8,128)(2,1)S(1)}, bf16[1,256,128,128]{3,2,1,0:T(8,128)(2,1)}, /*index=5*/s32[1,1]{1,0:T(1,128)}) %tuple.57), branch_computations={%region_1.1_spmd, %region_2.3_spmd} | conditional | flops 50728704 | bytes 13515284 | solution.py:36
  1694.4 6.7 fusion.4
  1702.2 25.4 %scatter_fusion = f32[256,6,128]{2,1,0:T(8,128)} fusion(f32[256,6,128]{2,1,0:T(8,128)} %broadcast.103, s32[256]{0:T(256)S(1)} %bitcast.26, f32[256,6,128]{2,1,0:T(8,128)S(1)} %fusion.4), kind=kCustom, calls=%fused_computation.1 | custom fusion | flops 196608 | bytes 2360320 | tf_op jit(solution)/shard_map/while/body/eval_jaxpr/cond/branch_1_fun/scatter-add | solution.py:20
  1727.6 2.1 convert_element_type.103
  1729.8 69.0 %reduce-scatter.2.cloned.1.call-done = bf16[16,6,128]{2,1,0:T(8,128)(2,1)} async-done(((bf16[256,6,128]{2,1,0:T(8,128)(2,1)}), bf16[16,6,128]{2,1,0:T(8,128)(2,1)}) %reduce-scatter.2.cloned.1.call-update) | async-done | bytes 24592 | tf_op jit(solution)/shard_map/while/body/eval_jaxpr/reduce_scatter | solution.py:56
  1800.2 1.6 collective-permute-done
  (212 shorter events, 53.6 us)
Async XLA Ops:
  7.4 112.7 %reduce-scatter.2.cloned.1.call-start = ((), (), s32[]{:S(2)}) async-start(), calls=%async_computation.1 | async-start | bytes 557056 | tf_op jit(solution)/shard_map/while/body/eval_jaxpr/reduce_scatter | solution.py:56
  7.5 3.2 copy-start
  120.8 2.2 collective-permute-start
  123.0 109.4 %reduce-scatter.2.cloned.1.call-start = ((), (), s32[]{:S(2)}) async-start(), calls=%async_computation.1 | async-start | bytes 557056 | tf_op jit(solution)/shard_map/while/body/eval_jaxpr/reduce_scatter | solution.py:56
  123.1 3.2 copy-start
  233.2 2.2 collective-permute-start
  235.4 110.6 %reduce-scatter.2.cloned.1.call-start = ((), (), s32[]{:S(2)}) async-start(), calls=%async_computation.1 | async-start | bytes 557056 | tf_op jit(solution)/shard_map/while/body/eval_jaxpr/reduce_scatter | solution.py:56
  235.5 3.2 copy-start
  346.8 2.2 collective-permute-start
  348.9 109.6 %reduce-scatter.2.cloned.1.call-start = ((), (), s32[]{:S(2)}) async-start(), calls=%async_computation.1 | async-start | bytes 557056 | tf_op jit(solution)/shard_map/while/body/eval_jaxpr/reduce_scatter | solution.py:56
  349.0 3.2 copy-start
  459.3 2.2 collective-permute-start
  461.5 109.1 %reduce-scatter.2.cloned.1.call-start = ((), (), s32[]{:S(2)}) async-start(), calls=%async_computation.1 | async-start | bytes 557056 | tf_op jit(solution)/shard_map/while/body/eval_jaxpr/reduce_scatter | solution.py:56
  461.6 3.2 copy-start
  571.4 2.2 collective-permute-start
  573.6 107.9 %reduce-scatter.2.cloned.1.call-start = ((), (), s32[]{:S(2)}) async-start(), calls=%async_computation.1 | async-start | bytes 557056 | tf_op jit(solution)/shard_map/while/body/eval_jaxpr/reduce_scatter | solution.py:56
  573.7 3.2 copy-start
  682.3 2.1 collective-permute-start
  684.5 108.3 %reduce-scatter.2.cloned.1.call-start = ((), (), s32[]{:S(2)}) async-start(), calls=%async_computation.1 | async-start | bytes 557056 | tf_op jit(solution)/shard_map/while/body/eval_jaxpr/reduce_scatter | solution.py:56
  684.5 3.2 copy-start
  793.6 2.2 collective-permute-start
  795.7 107.5 %reduce-scatter.2.cloned.1.call-start = ((), (), s32[]{:S(2)}) async-start(), calls=%async_computation.1 | async-start | bytes 557056 | tf_op jit(solution)/shard_map/while/body/eval_jaxpr/reduce_scatter | solution.py:56
  795.8 38.3 %copy-start = (s32[16,16]{1,0:T(8,128)S(1)}, s32[16,16]{1,0:T(8,128)}, u32[]{:S(2)}) copy-start(s32[16,16]{1,0:T(8,128)} %get-tuple-element.521) | copy-start | bytes 3076 | tf_op jit(solution)/shard_map/while
  904.0 2.2 collective-permute-start
  906.2 109.8 %reduce-scatter.2.cloned.1.call-start = ((), (), s32[]{:S(2)}) async-start(), calls=%async_computation.1 | async-start | bytes 557056 | tf_op jit(solution)/shard_map/while/body/eval_jaxpr/reduce_scatter | solution.py:56
  906.2 3.2 copy-start
  1016.8 2.2 collective-permute-start
  1019.0 109.3 %reduce-scatter.2.cloned.1.call-start = ((), (), s32[]{:S(2)}) async-start(), calls=%async_computation.1 | async-start | bytes 557056 | tf_op jit(solution)/shard_map/while/body/eval_jaxpr/reduce_scatter | solution.py:56
  1019.0 3.2 copy-start
  1129.1 2.2 collective-permute-start
  1131.3 110.5 %reduce-scatter.2.cloned.1.call-start = ((), (), s32[]{:S(2)}) async-start(), calls=%async_computation.1 | async-start | bytes 557056 | tf_op jit(solution)/shard_map/while/body/eval_jaxpr/reduce_scatter | solution.py:56
  1131.3 3.2 copy-start
  1242.6 2.2 collective-permute-start
  1244.7 109.5 %reduce-scatter.2.cloned.1.call-start = ((), (), s32[]{:S(2)}) async-start(), calls=%async_computation.1 | async-start | bytes 557056 | tf_op jit(solution)/shard_map/while/body/eval_jaxpr/reduce_scatter | solution.py:56
  1244.8 3.2 copy-start
  1355.1 2.2 collective-permute-start
  1357.3 109.1 %reduce-scatter.2.cloned.1.call-start = ((), (), s32[]{:S(2)}) async-start(), calls=%async_computation.1 | async-start | bytes 557056 | tf_op jit(solution)/shard_map/while/body/eval_jaxpr/reduce_scatter | solution.py:56
  1357.3 3.2 copy-start
  1467.1 2.2 collective-permute-start
  1469.3 107.8 %reduce-scatter.2.cloned.1.call-start = ((), (), s32[]{:S(2)}) async-start(), calls=%async_computation.1 | async-start | bytes 557056 | tf_op jit(solution)/shard_map/while/body/eval_jaxpr/reduce_scatter | solution.py:56
  1469.4 3.2 copy-start
  1578.0 2.2 collective-permute-start
  1580.2 108.3 %reduce-scatter.2.cloned.1.call-start = ((), (), s32[]{:S(2)}) async-start(), calls=%async_computation.1 | async-start | bytes 557056 | tf_op jit(solution)/shard_map/while/body/eval_jaxpr/reduce_scatter | solution.py:56
  1580.2 3.2 copy-start
  1689.2 2.2 collective-permute-start
  1691.4 107.4 %reduce-scatter.2.cloned.1.call-start = ((), (), s32[]{:S(2)}) async-start(), calls=%async_computation.1 | async-start | bytes 557056 | tf_op jit(solution)/shard_map/while/body/eval_jaxpr/reduce_scatter | solution.py:56
  1691.5 38.3 %copy-start = (s32[16,16]{1,0:T(8,128)S(1)}, s32[16,16]{1,0:T(8,128)}, u32[]{:S(2)}) copy-start(s32[16,16]{1,0:T(8,128)} %get-tuple-element.521) | copy-start | bytes 3076 | tf_op jit(solution)/shard_map/while
  1799.6 2.2 collective-permute-start
Sparse Core Ops, SparseCore 0:
  11.4 108.5 reduce-scatter.1
  127.0 105.3 reduce-scatter.1
  239.4 106.5 reduce-scatter.1
  352.6 105.8 reduce-scatter.1
  465.2 105.3 reduce-scatter.1
  577.3 104.1 reduce-scatter.1
  688.5 104.2 reduce-scatter.1
  834.2 68.9 reduce-scatter.1
  910.2 105.7 reduce-scatter.1
  1022.7 105.5 reduce-scatter.1
  1135.3 106.4 reduce-scatter.1
  1248.4 105.7 reduce-scatter.1
  1361.3 105.0 reduce-scatter.1
  1473.0 104.1 reduce-scatter.1
  1583.9 104.5 reduce-scatter.1
  1729.8 68.9 reduce-scatter.1
where the time goes:
time: 1810 us
  waiting for transfers between devices  1650 us (91%)
  other arithmetic  101 us (6%)
  local copies, waits for them, and re-layouts  21.3 us (1%)
    reduce_scatter x16, waiting for transfers between devices, reduce_terms(): lax.psum_scatter(partial_terms.astype(jnp.bfloat16), 'cols', scatter_dime...  1620 us
    scatter-add x2, other arithmetic, place(): buffer.at[target].add(terms * inside.astype(jnp.float32)[:, None, None])  50.8 us
  transfers between devices with their start and end apart: 32, of which 32 were waited for; matrix products, arithmetic and copies ran while one was open for 0% of the time, Pallas kernels for 0%

commit v1 on v0

v1 whole, which is shorter than its diff:
```python
import functools

import jax
import jax.numpy as jnp
from jax import lax
from jax.experimental import pallas as pl
from jax.experimental.pallas import tpu as pltpu
from jax.sharding import PartitionSpec as P

MESH = pl.DeviceIdType.MESH
CHUNKS = 8


def kernel(
    dims,
    cols_ref,
    count_ref,
    rows_ref,
    depth_ref,
    forcing_ref,
    tiles_ref,
    out_ref,
    tiles_v,
    x_rows,
    terms,
    pick,
    back_v,
    wet_v,
    send_v,
    recv_v,
    tile_sem,
    send_sem,
    recv_sem,
    back_send,
    back_recv,
):
    months, ncols, blk, tracers, block, slots, levels = dims
    deltas = (0, ncols - 1, 1, ncols // 2)
    ngroups = len(deltas)
    pad = x_rows.shape[1]
    per_chunk = slots // CHUNKS
    month = lax.axis_index("month")
    here = lax.axis_index("cols")
    earlier = lax.rem(month + months - 1, months)
    later = lax.rem(month + 1, months)
    last = months - 1

    def tile_copy(k):
        part = pl.ds(k * per_chunk, per_chunk)
        return pltpu.make_async_copy(tiles_ref.at[part], tiles_v.at[part], tile_sem.at[k])

    for k in range(CHUNKS):
        tile_copy(k).start()

    barrier = pltpu.get_barrier_semaphore()
    for other in (earlier, later):
        for delta in deltas:
            pl.semaphore_signal(
                barrier, inc=1,
                device_id={"month": other, "cols": lax.rem(here + delta, ncols)},
                device_id_type=MESH,
            )

    @pl.when(month == 0)
    def _():
        for delta in deltas[1:]:
            pl.semaphore_signal(
                barrier, inc=1,
                device_id={"month": month, "cols": lax.rem(here + delta, ncols)},
                device_id_type=MESH,
            )

    spread = (
        lax.broadcasted_iota(jnp.int32, (depth_ref.shape[1], block), 1) % depth_ref.shape[1]
        == lax.broadcasted_iota(jnp.int32, (depth_ref.shape[1], block), 0)
    ).astype(jnp.float32).astype(jnp.bfloat16)
    deep = jnp.dot(
        depth_ref[...].astype(jnp.float32).astype(jnp.bfloat16), spread,
        preferred_element_type=jnp.float32,
    )
    level = (lax.broadcasted_iota(jnp.int32, (blk, block), 1) // depth_ref.shape[1]).astype(jnp.float32)
    wet_v[...] = (level < deep).astype(jnp.float32)
    x_rows[...] = jnp.zeros_like(x_rows)
    live = lax.broadcasted_iota(jnp.int32, (blk, slots), 1) < count_ref[0, 0]
    inside = lax.broadcasted_iota(jnp.int32, (blk, slots), 0)
    for g, delta in enumerate(deltas):
        target = lax.rem(here + delta, ncols) * blk
        hit = ((inside + target) == rows_ref[...]) & live
        pick[g * blk:(g + 1) * blk, :] = hit.astype(jnp.float32).astype(jnp.bfloat16)

    def meet():
        @pl.when(month == 0)
        def _():
            pl.semaphore_wait(barrier, 3 * ngroups - 1)

        @pl.when(month != 0)
        def _():
            pl.semaphore_wait(barrier, 2 * ngroups)

    def set_x(x):
        x = x.astype(jnp.bfloat16).astype(jnp.float32)
        for t in range(tracers):
            x_rows[:, t, :] = x[t]

    def pair(g, swapped):
        s = 2 * g
        zero = jnp.zeros((pad, block), jnp.float32)
        xa = x_rows[cols_ref[0, s] & (blk - 1)]
        xb = x_rows[cols_ref[0, s + 1] & (blk - 1)]
        lhs = jnp.concatenate(
            [
                jnp.concatenate([xa, zero], 0).astype(jnp.bfloat16),
                jnp.concatenate([zero, xb], 0).astype(jnp.bfloat16),
            ], 1,
        )
        two = tiles_v[pl.ds(s, 2)]
        if swapped:
            out = jnp.dot(lhs, two.reshape(2 * block, block), preferred_element_type=jnp.float32)
        else:
            out = lax.dot_general(
                lhs, jnp.concatenate([two[0], two[1]], 1), (((1,), (1,)), ((), ())),
                preferred_element_type=jnp.float32,
            )
        terms[pl.ds(s * pad, 2 * pad), :] = out

    def link(sweep, g, target_month):
        slot = sweep + (month == 0).astype(jnp.int32)
        return pltpu.make_async_remote_copy(
            src_ref=send_v.at[sweep, g],
            dst_ref=recv_v.at[slot, g],
            send_sem=send_sem.at[sweep, g],
            recv_sem=recv_sem.at[slot, g],
            device_id={"month": target_month, "cols": lax.rem(here + deltas[g], ncols)},
            device_id_type=MESH,
        )

    def arrival(slot, g):
        return pltpu.make_async_remote_copy(
            src_ref=send_v.at[0, g],
            dst_ref=recv_v.at[slot, g],
            send_sem=send_sem.at[0, g],
            recv_sem=recv_sem.at[slot, g],
            device_id={"month": earlier, "cols": here},
            device_id_type=MESH,
        )

    def back(target_month):
        return pltpu.make_async_remote_copy(
            src_ref=back_v,
            dst_ref=out_ref,
            send_sem=back_send,
            recv_sem=back_recv,
            device_id={"month": target_month, "cols": here},
            device_id_type=MESH,
        )

    def gather_rows(sweep):
        for t in range(tracers):
            terms_t = terms[pl.ds(t, slots, stride=pad), :].astype(jnp.bfloat16)
            part = jnp.dot(pick[...], terms_t, preferred_element_type=jnp.float32)
            part = part.astype(jnp.bfloat16)
            for g in range(ngroups):
                send_v[sweep, g, t] = part[g * blk:(g + 1) * blk]

    def total(slot, own=None):
        parts = [recv_v[slot, g].astype(jnp.float32) for g in range(ngroups) if own is None or g]
        if own is not None:
            parts = [own.astype(jnp.float32)] + parts
        full = (parts[0] + parts[1]) + (parts[2] + parts[3])
        return full * wet_v[...][None]

    def turn_tiles(k):
        def one(i, carry):
            s = k * per_chunk + i
            tiles_v[s] = tiles_v[s].T
            return carry

        lax.fori_loop(0, per_chunk, one, 0, unroll=8)

    @pl.when(month == last)
    def _():
        set_x(forcing_ref[...])
        for k in range(CHUNKS):
            tile_copy(k).wait()

            def run(i, carry):
                pair(k * (per_chunk // 2) + i, False)
                return carry

            lax.fori_loop(0, per_chunk // 2, run, 0, unroll=per_chunk // 2)
        gather_rows(0)
        meet()
        for g in range(ngroups):
            link(0, g, earlier).start()

        for k in range(CHUNKS):
            turn_tiles(k)

    @pl.when(month != last)
    def _():
        meet()
        for k in range(CHUNKS):
            tile_copy(k).wait()
            turn_tiles(k)

    def sweep_step(sweep, carry):
        @pl.when((month != last) | (sweep > 0))
        def _():
            for g in range(ngroups):
                arrival(sweep, g).wait_recv()
            state = total(sweep)
            set_x(state + forcing_ref[...])

            def run(i, carry):
                pair(i, True)
                return carry

            lax.fori_loop(0, slots // 2, run, 0, unroll=slots // 2)
            gather_rows(sweep)

            @pl.when((month == 0) & (sweep > 0))
            def _():
                for g in range(1, ngroups):
                    link(sweep, g, month).start()

            @pl.when((month != 0) | (sweep == 0))
            def _():
                for g in range(ngroups):
                    link(sweep, g, earlier).start()

            @pl.when((month != last) & (sweep > 0))
            def _():
                back_v[...] = state
                back(later).start()

        return carry

    lax.fori_loop(0, 2, sweep_step, 0)

    @pl.when(month == 0)
    def _():
        for g in range(1, ngroups):
            arrival(2, g).wait_recv()
        out_ref[...] = total(2, send_v[1, 0])
        for g in range(ngroups):
            link(0, g, earlier).wait_send()
        for g in range(1, ngroups):
            link(1, g, month).wait_send()

    @pl.when(month != 0)
    def _():
        for sweep in range(2):
            for g in range(ngroups):
                link(sweep, g, earlier).wait_send()
        back(later).wait_recv()

    @pl.when(month != last)
    def _():
        back(later).wait_send()


def on_device(forcing, tiles, tile_rows, tile_cols, tile_count, depth):
    months = lax.axis_size("month")
    ncols = lax.axis_size("cols")
    _, blk, tracers, block = forcing.shape
    slots = tiles.shape[1]
    pad = 8
    levels = block // depth.shape[1]
    dims = (months, ncols, blk, tracers, block, slots, levels)
    vmem = pl.BlockSpec(memory_space=pltpu.VMEM)
    smem = pl.BlockSpec(memory_space=pltpu.SMEM)
    result = pl.pallas_call(
        functools.partial(kernel, dims),
        out_shape=jax.ShapeDtypeStruct((tracers, blk, block), jnp.float32),
        in_specs=[smem, smem, vmem, vmem, vmem, pl.BlockSpec(memory_space=pltpu.HBM)],
        out_specs=vmem,
        scratch_shapes=[
            pltpu.VMEM((slots, block, block), jnp.bfloat16),
            pltpu.VMEM((blk, pad, block), jnp.float32),
            pltpu.VMEM((slots * pad, block), jnp.float32),
            pltpu.VMEM((4 * blk, slots), jnp.bfloat16),
            pltpu.VMEM((tracers, blk, block), jnp.float32),
            pltpu.VMEM((blk, block), jnp.float32),
            pltpu.VMEM((2, 4, tracers, blk, block), jnp.bfloat16),
            pltpu.VMEM((3, 4, tracers, blk, block), jnp.bfloat16),
            pltpu.SemaphoreType.DMA((CHUNKS,)),
            pltpu.SemaphoreType.DMA((2, 4)),
            pltpu.SemaphoreType.DMA((3, 4)),
            pltpu.SemaphoreType.DMA,
            pltpu.SemaphoreType.DMA,
        ],
        compiler_params=pltpu.CompilerParams(
            collective_id=0, has_side_effects=True, vmem_limit_bytes=56 << 20
        ),
        name="year_sweeps",
    )(tile_cols, tile_count, tile_rows, depth, jnp.swapaxes(forcing[0], 0, 1), tiles[0])
    return jnp.swapaxes(result, 0, 1)[None]


def solution(mesh):
    in_specs = (
        P("month", "cols", None, None),
        P("month", "cols", None, None),
        P("month", "cols"),
        P("month", "cols"),
        P("month", "cols"),
        P("cols", None),
    )
    out_specs = P("month", "cols", None, None)
    return jax.shard_map(
        on_device, mesh=mesh, in_specs=in_specs, out_specs=out_specs, check_vma=False
    )
```

time: 1810 us -> 104 us (0.06)
  waiting for transfers between devices: 1650 us -> 0 us
  Pallas kernels: 0 us -> 101 us
  other arithmetic: 101 us -> 0 us
  local copies, waits for them, and re-layouts: 21.3 us -> 1.42 us
    reduce_scatter x16 -> x0, waiting for transfers between devices: 1620 us -> none  [reduce_terms(): lax.psum_scatter(partial_terms.astype(jnp.bfloat16), 'cols', scatter_dime...]
    pallas_call x0 -> x1, Pallas kernels: none -> 101 us  [on_device(): pl.pallas_call(functools.partial(kernel, dims), out_shape=jax.ShapeDtypeS...]
    scatter-add x2 -> x0, other arithmetic: 50.8 us -> none  [place(): buffer.at[target].add(terms * inside.astype(jnp.float32)[:, None, None])]
    convert_element_type x50 -> x0, other arithmetic: 35.1 us -> none  [the longest x16 33.5 us: reduce_terms(): partial_terms.astype(jnp.bfloat16)]
    ppermute x16 -> x0, waiting for transfers between devices: 25.6 us -> none  [from_behind(): lax.ppermute(shard, axis, [(i, (i + by) % length) for i in range(length)])]
    another operation x48 -> x0, local copies, waits for them, and re-layouts: 18.1 us -> none
  transfers between devices with their start and end apart: 32 -> 0, of which waited for: 32 -> 0; matrix products, arithmetic and copies ran while one was open for 0% -> 0% of each run, Pallas kernels for 0% -> 0%
where the time goes in v1:
time: 104 us; the launch traced here: 103 us
  Pallas kernels  101 us (97%)
  local copies, waits for them, and re-layouts  1.42 us (1%)
    pallas_call x1, Pallas kernels, on_device(): pl.pallas_call(functools.partial(kernel, dims), out_shape=jax.ShapeDtypeS...  101 us

profile of v1, /device:TPU:0, one launch (start us, length us, event | category | flops | bytes accessed | tf_op | source)
XLA Modules:
  0.0 103.5 jit_solution(678307201663867176)
XLA Ops:
  0.7 101.4 %year_sweeps.1 = f32[6,16,128]{2,1,0:T(8,128)} custom-call(s32[1,256]{1,0:T(1,128)} %cols_ref.1, s32[1,1]{1,0:T(1,128)S(6)} %copy.8.count_ref, s32[1,256]{1,0:T(1,128)} %rows_ref.1, s32[16,16]{1,0:T(8,128)} %depth_ref.1, f32[6,16,128]{2,1,0:T(8,128)} %bitcast.9, bf16[256,128,128]{2,1,0:T(8,128)(2,1)} %bitcast.7), custom_call_target="tpu_custom_call" | custom-call | tf_op jit(solution)/shard_map/year_sweeps/pallas_call | solution.py:272
  102.0 1.4 %copy.9 = f32[1,16,6,128]{3,1,2,0:T(8,128)} copy(f32[1,16,6,128]{3,1,2,0:T(8,128)} %bitcast.8) | data formatting | bytes 98304

commit v2 on v1

--- a/solution.py
+++ b/solution.py
@@ -9,6 +9,7 @@
 
 MESH = pl.DeviceIdType.MESH
 CHUNKS = 8
+HALVES = 2
 
 
 def kernel(
@@ -38,6 +39,7 @@
     deltas = (0, ncols - 1, 1, ncols // 2)
     ngroups = len(deltas)
     pad = x_rows.shape[1]
+    part = tracers // HALVES
     per_chunk = slots // CHUNKS
     month = lax.axis_index("month")
     here = lax.axis_index("cols")
@@ -53,22 +55,25 @@
         tile_copy(k).start()
 
     barrier = pltpu.get_barrier_semaphore()
-    for other in (earlier, later):
-        for delta in deltas:
-            pl.semaphore_signal(
-                barrier, inc=1,
-                device_id={"month": other, "cols": lax.rem(here + delta, ncols)},
-                device_id_type=MESH,
-            )
+
+    def greet(other_month, delta):
+        pl.semaphore_signal(
+            barrier, inc=1,
+            device_id={"month": other_month, "cols": lax.rem(here + delta, ncols)},
+            device_id_type=MESH,
+        )
+
+    for delta in deltas:
+        greet(later, delta)
 
     @pl.when(month == 0)
     def _():
         for delta in deltas[1:]:
-            pl.semaphore_signal(
-                barrier, inc=1,
-                device_id={"month": month, "cols": lax.rem(here + delta, ncols)},
-                device_id_type=MESH,
-            )
+            greet(month, delta)
+
+    @pl.when(month != 0)
+    def _():
+        greet(earlier, 0)
 
     spread = (
         lax.broadcasted_iota(jnp.int32, (depth_ref.shape[1], block), 1) % depth_ref.shape[1]
@@ -91,15 +96,19 @@
     def meet():
         @pl.when(month == 0)
         def _():
-            pl.semaphore_wait(barrier, 3 * ngroups - 1)
-
-        @pl.when(month != 0)
-        def _():
             pl.semaphore_wait(barrier, 2 * ngroups)
+
+        @pl.when(month == last)
+        def _():
+            pl.semaphore_wait(barrier, ngroups)
+
+        @pl.when((month != 0) & (month != last))
+        def _():
+            pl.semaphore_wait(barrier, ngroups + 1)
 
     def set_x(x):
         x = x.astype(jnp.bfloat16).astype(jnp.float32)
-        for t in range(tracers):
+        for t in range(x.shape[0]):
             x_rows[:, t, :] = x[t]
 
     def pair(g, swapped):
@@ -123,50 +132,65 @@
             )
         terms[pl.ds(s * pad, 2 * pad), :] = out
 
-    def link(sweep, g, target_month):
+    def link(sweep, half, g, target_month):
         slot = sweep + (month == 0).astype(jnp.int32)
         return pltpu.make_async_remote_copy(
-            src_ref=send_v.at[sweep, g],
-            dst_ref=recv_v.at[slot, g],
-            send_sem=send_sem.at[sweep, g],
-            recv_sem=recv_sem.at[slot, g],
+            src_ref=send_v.at[sweep, half, g],
+            dst_ref=recv_v.at[slot, half, g],
+            send_sem=send_sem.at[sweep, half, g],
+            recv_sem=recv_sem.at[slot, half, g],
             device_id={"month": target_month, "cols": lax.rem(here + deltas[g], ncols)},
             device_id_type=MESH,
         )
 
-    def arrival(slot, g):
+    def arrival(slot, half, g):
         return pltpu.make_async_remote_copy(
-            src_ref=send_v.at[0, g],
-            dst_ref=recv_v.at[slot, g],
-            send_sem=send_sem.at[0, g],
-            recv_sem=recv_sem.at[slot, g],
+            src_ref=send_v.at[0, half, g],
+            dst_ref=recv_v.at[slot, half, g],
+            send_sem=send_sem.at[0, half, g],
+            recv_sem=recv_sem.at[slot, half, g],
             device_id={"month": earlier, "cols": here},
             device_id_type=MESH,
         )
 
-    def back(target_month):
+    def send_all(sweep, half, target_month, groups):
+        near_end = lax.rem(here, 4) == 3
+
+        @pl.when(near_end)
+        def _():
+            for g in (2, 3, 1, 0):
+                if g in groups:
+                    link(sweep, half, g, target_month).start()
+
+        @pl.when(jnp.logical_not(near_end))
+        def _():
+            for g in (1, 3, 2, 0):
+                if g in groups:
+                    link(sweep, half, g, target_month).start()
+
+    def back(half):
         return pltpu.make_async_remote_copy(
-            src_ref=back_v,
-            dst_ref=out_ref,
-            send_sem=back_send,
-            recv_sem=back_recv,
-            device_id={"month": target_month, "cols": here},
+            src_ref=back_v.at[half],
+            dst_ref=out_ref.at[pl.ds(half * part, part)],
+            send_sem=back_send.at[half],
+            recv_sem=back_recv.at[half],
+            device_id={"month": later, "cols": here},
             device_id_type=MESH,
         )
 
-    def gather_rows(sweep):
-        for t in range(tracers):
-            terms_t = terms[pl.ds(t, slots, stride=pad), :].astype(jnp.bfloat16)
-            part = jnp.dot(pick[...], terms_t, preferred_element_type=jnp.float32)
-            part = part.astype(jnp.bfloat16)
+    def gather_rows(sweep, half, first):
+        for t in range(part):
+            terms_t = terms[pl.ds(first + t, slots, stride=pad), :].astype(jnp.bfloat16)
+            rows_t = jnp.dot(pick[...], terms_t, preferred_element_type=jnp.float32)
+            rows_t = rows_t.astype(jnp.bfloat16)
             for g in range(ngroups):
-                send_v[sweep, g, t] = part[g * blk:(g + 1) * blk]
-
-    def total(slot, own=None):
-        parts = [recv_v[slot, g].astype(jnp.float32) for g in range(ngroups) if own is None or g]
+                send_v[sweep, half, g, t] = rows_t[g * blk:(g + 1) * blk]
+
+    def total(slot, half, own=None):
+        got = [recv_v[slot, half, g].astype(jnp.float32) for g in range(ngroups) if own is None or g]
         if own is not None:
-            parts = [own.astype(jnp.float32)] + parts
-        full = (parts[0] + parts[1]) + (parts[2] + parts[3])
+            got = [own.astype(jnp.float32)] + got
+        full = (got[0] + got[1]) + (got[2] + got[3])
         return full * wet_v[...][None]
 
     def turn_tiles(k):
@@ -188,10 +212,11 @@
                 return carry
 
             lax.fori_loop(0, per_chunk // 2, run, 0, unroll=per_chunk // 2)
-        gather_rows(0)
-        meet()
-        for g in range(ngroups):
-            link(0, g, earlier).start()
+        for half in range(HALVES):
+            gather_rows(0, half, half * part)
+            if half == 0:
+                meet()
+            send_all(0, half, earlier, range(ngroups))
 
         for k in range(CHUNKS):
             turn_tiles(k)
@@ -203,60 +228,64 @@
             tile_copy(k).wait()
             turn_tiles(k)
 
-    def sweep_step(sweep, carry):
+    def step(k, carry):
+        sweep, half = k // HALVES, lax.rem(k, HALVES)
+
         @pl.when((month != last) | (sweep > 0))
         def _():
             for g in range(ngroups):
-                arrival(sweep, g).wait_recv()
-            state = total(sweep)
-            set_x(state + forcing_ref[...])
+                arrival(sweep, half, g).wait_recv()
+            state = total(sweep, half)
+            set_x(state + forcing_ref[pl.ds(half * part, part)])
 
             def run(i, carry):
                 pair(i, True)
                 return carry
 
             lax.fori_loop(0, slots // 2, run, 0, unroll=slots // 2)
-            gather_rows(sweep)
+            gather_rows(sweep, half, 0)
 
             @pl.when((month == 0) & (sweep > 0))
             def _():
-                for g in range(1, ngroups):
-                    link(sweep, g, month).start()
+                send_all(sweep, half, month, range(1, ngroups))
 
             @pl.when((month != 0) | (sweep == 0))
             def _():
-                for g in range(ngroups):
-                    link(sweep, g, earlier).start()
+                send_all(sweep, half, earlier, range(ngroups))
 
             @pl.when((month != last) & (sweep > 0))
             def _():
-                back_v[...] = state
-                back(later).start()
+                back_v[half] = total(sweep, half)
+                back(half).start()
 
         return carry
 
-    lax.fori_loop(0, 2, sweep_step, 0)
+    lax.fori_loop(0, 2 * HALVES, step, 0)
 
     @pl.when(month == 0)
     def _():
-        for g in range(1, ngroups):
-            arrival(2, g).wait_recv()
-        out_ref[...] = total(2, send_v[1, 0])
-        for g in range(ngroups):
-            link(0, g, earlier).wait_send()
-        for g in range(1, ngroups):
-            link(1, g, month).wait_send()
+        for half in range(HALVES):
+            for g in range(1, ngroups):
+                arrival(2, half, g).wait_recv()
+            out_ref[half * part:(half + 1) * part] = total(2, half, send_v[1, half, 0])
+        for half in range(HALVES):
+            for g in range(ngroups):
+                link(0, half, g, earlier).wait_send()
+            for g in range(1, ngroups):
+                link(1, half, g, month).wait_send()
 
     @pl.when(month != 0)
     def _():
-        for sweep in range(2):
-            for g in range(ngroups):
-                link(sweep, g, earlier).wait_send()
-        back(later).wait_recv()
+        for half in range(HALVES):
+            for sweep in range(2):
+                for g in range(ngroups):
+                    link(sweep, half, g, earlier).wait_send()
+            back(half).wait_recv()
 
     @pl.when(month != last)
     def _():
-        back(later).wait_send()
+        for half in range(HALVES):
+            back(half).wait_send()
 
 
 def on_device(forcing, tiles, tile_rows, tile_cols, tile_count, depth):
@@ -265,6 +294,7 @@
     _, blk, tracers, block = forcing.shape
     slots = tiles.shape[1]
     pad = 8
+    part = tracers // HALVES
     levels = block // depth.shape[1]
     dims = (months, ncols, blk, tracers, block, slots, levels)
     vmem = pl.BlockSpec(memory_space=pltpu.VMEM)
@@ -279,15 +309,15 @@
             pltpu.VMEM((blk, pad, block), jnp.float32),
             pltpu.VMEM((slots * pad, block), jnp.float32),
             pltpu.VMEM((4 * blk, slots), jnp.bfloat16),
-            pltpu.VMEM((tracers, blk, block), jnp.float32),
+            pltpu.VMEM((HALVES, part, blk, block), jnp.float32),
             pltpu.VMEM((blk, block), jnp.float32),
-            pltpu.VMEM((2, 4, tracers, blk, block), jnp.bfloat16),
-            pltpu.VMEM((3, 4, tracers, blk, block), jnp.bfloat16),
+            pltpu.VMEM((2, HALVES, 4, part, blk, block), jnp.bfloat16),
+            pltpu.VMEM((3, HALVES, 4, part, blk, block), jnp.bfloat16),
             pltpu.SemaphoreType.DMA((CHUNKS,)),
-            pltpu.SemaphoreType.DMA((2, 4)),
-            pltpu.SemaphoreType.DMA((3, 4)),
-            pltpu.SemaphoreType.DMA,
-            pltpu.SemaphoreType.DMA,
+            pltpu.SemaphoreType.DMA((2, HALVES, 4)),
+            pltpu.SemaphoreType.DMA((3, HALVES, 4)),
+            pltpu.SemaphoreType.DMA((HALVES,)),
+            pltpu.SemaphoreType.DMA((HALVES,)),
         ],
         compiler_params=pltpu.CompilerParams(
             collective_id=0, has_side_effects=True, vmem_limit_bytes=56 << 20

time: 104 us -> 102 us (0.981)
  Pallas kernels: 101 us -> 99.6 us
    pallas_call x1, Pallas kernels: 101 us -> 99.6 us  [on_device(): pl.pallas_call(functools.partial(kernel, dims), out_shape=jax.ShapeDtypeS...]
where the time goes in v2:
time: 102 us
  Pallas kernels  99.6 us (98%)
  local copies, waits for them, and re-layouts  1.42 us (1%)
    pallas_call x1, Pallas kernels, on_device(): pl.pallas_call(functools.partial(kernel, dims), out_shape=jax.ShapeDtypeS...  99.6 us

profile of v2, /device:TPU:0, one launch (start us, length us, event | category | flops | bytes accessed | tf_op | source)
XLA Modules:
  0.0 101.7 jit_solution(13103600600550058907)
XLA Ops:
  0.7 99.6 %year_sweeps.1 = f32[6,16,128]{2,1,0:T(8,128)} custom-call(s32[1,256]{1,0:T(1,128)} %cols_ref.1, s32[1,1]{1,0:T(1,128)S(6)} %copy.8.count_ref, s32[1,256]{1,0:T(1,128)} %rows_ref.1, s32[16,16]{1,0:T(8,128)} %depth_ref.1, f32[6,16,128]{2,1,0:T(8,128)} %bitcast.9, bf16[256,128,128]{2,1,0:T(8,128)(2,1)} %bitcast.7), custom_call_target="tpu_custom_call" | custom-call | tf_op jit(solution)/shard_map/year_sweeps/pallas_call | solution.py:302
  100.3 1.4 %copy.9 = f32[1,16,6,128]{3,1,2,0:T(8,128)} copy(f32[1,16,6,128]{3,1,2,0:T(8,128)} %bitcast.8) | data formatting | bytes 98304

commit v3 on v2

v3 whole, which is shorter than its diff:
```python
import functools

import jax
import jax.numpy as jnp
from jax import lax
from jax.experimental import pallas as pl
from jax.experimental.pallas import tpu as pltpu
from jax.sharding import PartitionSpec as P

MESH = pl.DeviceIdType.MESH
CHUNKS = 8
HALVES = 2


def kernel(
    dims,
    cols_ref,
    count_ref,
    rows_ref,
    depth_ref,
    forcing_ref,
    tiles_ref,
    out_ref,
    tiles_v,
    x_rows,
    terms,
    pick,
    force_v,
    wet_v,
    back_v,
    send_v,
    recv_v,
    cols_v,
    cols_w,
    tile_sem,
    send_sem,
    recv_sem,
    back_send,
    back_recv,
    hand_send,
    hand_recv,
    table_send,
    table_recv,
    cols_sem,
):
    months, ncols, blk, tracers, block, slots = dims
    deltas = (0, ncols - 1, 1, ncols // 2)
    ngroups = len(deltas)
    everyone = tuple(range(ngroups))
    pad = x_rows.shape[1]
    part = tracers // HALVES
    per_chunk = slots // CHUNKS
    month = lax.axis_index("month")
    here = lax.axis_index("cols")
    last = months - 1
    odd = lax.rem(month, 2) == 1
    even = jnp.logical_not(odd)

    def tile_copy(k):
        rows = pl.ds(k * per_chunk, per_chunk)
        return pltpu.make_async_copy(tiles_ref.at[rows], tiles_v.at[0, rows], tile_sem.at[k])

    for k in range(CHUNKS):
        tile_copy(k).start()
    own_cols = pltpu.make_async_copy(cols_ref, cols_v.at[0], cols_sem)
    own_cols.start()

    barrier = pltpu.get_barrier_semaphore()

    def greet(other_month, groups):
        for g in groups:
            pl.semaphore_signal(
                barrier, inc=1,
                device_id={"month": other_month, "cols": lax.rem(here + deltas[g], ncols)},
                device_id_type=MESH,
            )

    @pl.when(odd)
    def _():
        greet(lax.rem(month + 2, months), everyone)
        greet(month, everyone[1:])
        greet(month - 1, (0,))

    @pl.when(month == last - 2)
    def _():
        greet(last - 1, everyone)

    @pl.when(month == last - 1)
    def _():
        greet(last, everyone)

    @pl.when(month == 0)
    def _():
        greet(1, everyone)

    @pl.when(even & (month > 0))
    def _():
        greet(month - 1, (0,))

    def meet():
        cases = (
            (month == 1, 3 * ngroups),
            (odd & (month > 1) & (month < last), 2 * ngroups),
            (month == last, 3 * ngroups - 1),
            (month == last - 1, ngroups + 1),
            (even & (month < last - 1), 1),
        )
        for case, peers in cases:
            @pl.when(case)
            def _():
                pl.semaphore_wait(barrier, peers)

    spread = (
        lax.broadcasted_iota(jnp.int32, (depth_ref.shape[1], block), 1) % depth_ref.shape[1]
        == lax.broadcasted_iota(jnp.int32, (depth_ref.shape[1], block), 0)
    ).astype(jnp.float32).astype(jnp.bfloat16)
    deep = jnp.dot(
        depth_ref[...].astype(jnp.float32).astype(jnp.bfloat16), spread,
        preferred_element_type=jnp.float32,
    )
    level = (lax.broadcasted_iota(jnp.int32, (blk, block), 1) // depth_ref.shape[1]).astype(jnp.float32)
    wet_v[...] = (level < deep).astype(jnp.float32)
    force_v[0] = forcing_ref[...]
    x_rows[...] = jnp.zeros_like(x_rows)
    live = lax.broadcasted_iota(jnp.int32, (blk, slots), 1) < count_ref[0, 0]
    inside = lax.broadcasted_iota(jnp.int32, (blk, slots), 0)
    for g, delta in enumerate(deltas):
        target = lax.rem(here + delta, ncols) * blk
        hit = ((inside + target) == rows_ref[...]) & live
        pick[0, g * blk:(g + 1) * blk, :] = hit.astype(jnp.float32).astype(jnp.bfloat16)
    own_cols.wait()

    def set_x(x):
        x = x.astype(jnp.bfloat16).astype(jnp.float32)
        for t in range(x.shape[0]):
            x_rows[:, t, :] = x[t]

    def pair(g, held, swapped):
        s = 2 * g
        zero = jnp.zeros((pad, block), jnp.float32)
        xa = x_rows[cols_v[held, 0, s] & (blk - 1)]
        xb = x_rows[cols_v[held, 0, s + 1] & (blk - 1)]
        lhs = jnp.concatenate(
            [
                jnp.concatenate([xa, zero], 0).astype(jnp.bfloat16),
                jnp.concatenate([zero, xb], 0).astype(jnp.bfloat16),
            ], 1,
        )
        two = tiles_v[held, pl.ds(s, 2)]
        if swapped:
            out = jnp.dot(lhs, two.reshape(2 * block, block), preferred_element_type=jnp.float32)
        else:
            out = lax.dot_general(
                lhs, jnp.concatenate([two[0], two[1]], 1), (((1,), (1,)), ((), ())),
                preferred_element_type=jnp.float32,
            )
        terms[pl.ds(s * pad, 2 * pad), :] = out

    def link(turn, half, g, target_month, slot):
        return pltpu.make_async_remote_copy(
            src_ref=send_v.at[turn, half, g],
            dst_ref=recv_v.at[slot, half, g],
            send_sem=send_sem.at[turn, half, g],
            recv_sem=recv_sem.at[slot, half, g],
            device_id={"month": target_month, "cols": lax.rem(here + deltas[g], ncols)},
            device_id_type=MESH,
        )

    other = lax.rem(month + 2, months)

    def send_all(turn, half, target_month, slot, groups):
        near_end = lax.rem(here, 4) == 3

        @pl.when(near_end)
        def _():
            for g in (2, 3, 1, 0):
                if g in groups:
                    link(turn, half, g, target_month, slot).start()

        @pl.when(jnp.logical_not(near_end))
        def _():
            for g in (1, 3, 2, 0):
                if g in groups:
                    link(turn, half, g, target_month, slot).start()

    def back(half):
        return pltpu.make_async_remote_copy(
            src_ref=back_v.at[half],
            dst_ref=out_ref.at[pl.ds(half * part, part)],
            send_sem=back_send.at[half],
            recv_sem=back_recv.at[half],
            device_id={"month": lax.rem(month + 1, months), "cols": here},
            device_id_type=MESH,
        )

    def hand(source, dest, send, recv):
        return pltpu.make_async_remote_copy(
            src_ref=source, dst_ref=dest, send_sem=send, recv_sem=recv,
            device_id={"month": lax.rem(month + 1, months), "cols": here},
            device_id_type=MESH,
        )

    def hand_tiles(k):
        rows = pl.ds(k * per_chunk, per_chunk)
        return hand(tiles_v.at[0, rows], tiles_v.at[1, rows], hand_send.at[k], hand_recv.at[k])

    def hand_tables():
        return (
            hand(pick.at[0], pick.at[1], table_send.at[0], table_recv.at[0]),
            hand(force_v.at[0], force_v.at[1], table_send.at[1], table_recv.at[1]),
            hand(cols_ref, cols_w, table_send.at[2], table_recv.at[2]),
        )

    def gather_rows(held, turn, half, first):
        for t in range(part):
            terms_t = terms[pl.ds(first + t, slots, stride=pad), :].astype(jnp.bfloat16)
            rows_t = jnp.dot(pick[held], terms_t, preferred_element_type=jnp.float32)
            rows_t = rows_t.astype(jnp.bfloat16)
            for g in range(ngroups):
                send_v[turn, half, g, t] = rows_t[g * blk:(g + 1) * blk]

    def total(slot, half):
        got = [recv_v[slot, half, g].astype(jnp.float32) for g in range(ngroups)]
        full = (got[0] + got[1]) + (got[2] + got[3])
        return full * wet_v[...][None]

    def turn_tiles(k):
        def one(i, carry):
            s = k * per_chunk + i
            tiles_v[0, s] = tiles_v[0, s].T
            return carry

        lax.fori_loop(0, per_chunk, one, 0, unroll=8)

    @pl.when(month == last)
    def _():
        set_x(force_v[0])
        for k in range(CHUNKS):
            tile_copy(k).wait()

            def run(i, carry):
                pair(k * (per_chunk // 2) + i, 0, False)
                return carry

            lax.fori_loop(0, per_chunk // 2, run, 0, unroll=per_chunk // 2)
        for half in range(HALVES):
            gather_rows(0, 0, half, half * part)
            if half == 0:
                meet()
            send_all(0, half, last - 1, 0, everyone)

        for k in range(CHUNKS):
            turn_tiles(k)

    @pl.when(month == last - 1)
    def _():
        for k in range(CHUNKS):
            tile_copy(k).wait()
            turn_tiles(k)
        meet()
        for copy in hand_tables():
            copy.start()

    @pl.when(even & (month < last - 1))
    def _():
        for k in range(CHUNKS):
            tile_copy(k).wait()
            turn_tiles(k)
            if k == 0:
                meet()
                for copy in hand_tables():
                    copy.start()
            hand_tiles(k).start()

    @pl.when(odd & (month < last))
    def _():
        for k in range(CHUNKS):
            tile_copy(k).wait()
            turn_tiles(k)
        meet()

    def step(k, carry):
        sweep = k // (2 * HALVES)
        held = lax.rem(k // HALVES, 2)
        half = lax.rem(k, HALVES)
        turn = 2 * sweep + held
        opening = (month == last) & (sweep == 0)
        spare = (month == last - 1) & (turn == 0)
        took = jnp.where(month == last, 1, 0)

        @pl.when(odd & (held == 1) & (half == 0) & (sweep == took))
        def _():
            for copy in hand_tables():
                copy.wait_recv()
            pair_cols = pltpu.make_async_copy(cols_w, cols_v.at[1], cols_sem)
            pair_cols.start()
            for c in range(CHUNKS):
                hand_tiles(c).wait_recv()
            pair_cols.wait()

        @pl.when((odd & jnp.logical_not(opening)) | spare)
        def _():
            @pl.when(held == 0)
            def _():
                link(turn, half, 0, other, turn).wait_recv()

            @pl.when(held == 1)
            def _():
                recv_v[turn, half, 0] = send_v[turn - held, half, 0]

            for g in range(1, ngroups):
                link(turn, half, g, other, turn).wait_recv()
            state = total(turn, half)
            set_x(state + force_v[held, pl.ds(half * part, part)])

            def run(i, carry):
                pair(i, held, True)
                return carry

            lax.fori_loop(0, slots // 2, run, 0, unroll=slots // 2)
            gather_rows(held, turn, half, 0)

            @pl.when(spare)
            def _():
                send_all(turn, half, month - 1, 0, everyone)

            @pl.when(odd & (held == 0))
            def _():
                send_all(turn, half, month, turn + 1, everyone[1:])

            @pl.when(odd & (held == 1) & ((month > 1) | (sweep == 0)))
            def _():
                ahead = jnp.where(month == 1, 2, 0)
                send_all(turn, half, lax.rem(month + months - 2, months), 2 * sweep + ahead, everyone)

            @pl.when(odd & (held == 1) & (month == 1) & (sweep == 1))
            def _():
                send_all(turn, half, 0, 0, everyone)

            @pl.when((sweep == 1) & (held == 1))
            def _():
                out_ref[pl.ds(half * part, part)] = total(turn, half)

            @pl.when((sweep == 1) & (held == 0) & (month < last))
            def _():
                back_v[half] = total(turn, half)
                back(half).start()

        return carry

    lax.fori_loop(0, 4 * HALVES, step, 0)

    @pl.when(month == last - 1)
    def _():
        for k in range(CHUNKS):
            hand_tiles(k).start()

    @pl.when(month == 0)
    def _():
        for half in range(HALVES):
            for g in range(ngroups):
                link(0, half, g, other, 0).wait_recv()
            out_ref[half * part:(half + 1) * part] = total(0, half)

    @pl.when(even)
    def _():
        for copy in hand_tables():
            copy.wait_send()
        for k in range(CHUNKS):
            hand_tiles(k).wait_send()

    @pl.when(even & (month > 0))
    def _():
        for half in range(HALVES):
            back(half).wait_recv()

    @pl.when((month == last - 1) | (month == last))
    def _():
        for half in range(HALVES):
            for g in range(ngroups):
                link(0, half, g, other, 0).wait_send()

    @pl.when(odd & (month < last))
    def _():
        for half in range(HALVES):
            back(half).wait_send()
            for g in range(1, ngroups):
                link(0, half, g, other, 0).wait_send()
            for g in range(ngroups):
                link(1, half, g, other, 0).wait_send()

    @pl.when(odd)
    def _():
        for half in range(HALVES):
            for g in range(1, ngroups):
                link(2, half, g, other, 0).wait_send()
            for g in range(ngroups):
                link(3, half, g, other, 0).wait_send()


def on_device(forcing, tiles, tile_rows, tile_cols, tile_count, depth):
    months = lax.axis_size("month")
    ncols = lax.axis_size("cols")
    _, blk, tracers, block = forcing.shape
    slots = tiles.shape[1]
    pad = 8
    part = tracers // HALVES
    dims = (months, ncols, blk, tracers, block, slots)
    vmem = pl.BlockSpec(memory_space=pltpu.VMEM)
    smem = pl.BlockSpec(memory_space=pltpu.SMEM)
    result = pl.pallas_call(
        functools.partial(kernel, dims),
        out_shape=jax.ShapeDtypeStruct((tracers, blk, block), jnp.float32),
        in_specs=[vmem, smem, vmem, vmem, vmem, pl.BlockSpec(memory_space=pltpu.HBM)],
        out_specs=vmem,
        scratch_shapes=[
            pltpu.VMEM((2, slots, block, block), jnp.bfloat16),
            pltpu.VMEM((blk, pad, block), jnp.float32),
            pltpu.VMEM((slots * pad, block), jnp.float32),
            pltpu.VMEM((2, 4 * blk, slots), jnp.bfloat16),
            pltpu.VMEM((2, tracers, blk, block), jnp.float32),
            pltpu.VMEM((blk, block), jnp.float32),
            pltpu.VMEM((HALVES, part, blk, block), jnp.float32),
            pltpu.VMEM((4, HALVES, 4, part, blk, block), jnp.bfloat16),
            pltpu.VMEM((4, HALVES, 4, part, blk, block), jnp.bfloat16),
            pltpu.SMEM((2, 1, slots), jnp.int32),
            pltpu.VMEM((1, slots), jnp.int32),
            pltpu.SemaphoreType.DMA((CHUNKS,)),
            pltpu.SemaphoreType.DMA((4, HALVES, 4)),
            pltpu.SemaphoreType.DMA((4, HALVES, 4)),
            pltpu.SemaphoreType.DMA((HALVES,)),
            pltpu.SemaphoreType.DMA((HALVES,)),
            pltpu.SemaphoreType.DMA((CHUNKS,)),
            pltpu.SemaphoreType.DMA((CHUNKS,)),
            pltpu.SemaphoreType.DMA((3,)),
            pltpu.SemaphoreType.DMA((3,)),
            pltpu.SemaphoreType.DMA,
        ],
        compiler_params=pltpu.CompilerParams(
            collective_id=0, has_side_effects=True, vmem_limit_bytes=56 << 20
        ),
        name="year_sweeps",
    )(tile_cols, tile_count, tile_rows, depth, jnp.swapaxes(forcing[0], 0, 1), tiles[0])
    return jnp.swapaxes(result, 0, 1)[None]


def solution(mesh):
    in_specs = (
        P("month", "cols", None, None),
        P("month", "cols", None, None),
        P("month", "cols"),
        P("month", "cols"),
        P("month", "cols"),
        P("cols", None),
    )
    out_specs = P("month", "cols", None, None)
    return jax.shard_map(
        on_device, mesh=mesh, in_specs=in_specs, out_specs=out_specs, check_vma=False
    )
```

time: 102 us -> 96.6 us (0.947)
  Pallas kernels: 99.6 us -> 94.2 us
    pallas_call x1, Pallas kernels: 99.6 us -> 94.2 us  [on_device(): pl.pallas_call(functools.partial(kernel, dims), out_shape=jax.ShapeDtypeS...]
where the time goes in v3:
time: 96.6 us; the launch traced here: 96.3 us
  Pallas kernels  94.2 us (98%)
  local copies, waits for them, and re-layouts  1.42 us (1%)
    pallas_call x1, Pallas kernels, on_device(): pl.pallas_call(functools.partial(kernel, dims), out_shape=jax.ShapeDtypeS...  94.2 us

profile of v3, /device:TPU:0, one launch (start us, length us, event | category | flops | bytes accessed | tf_op | source)
XLA Modules:
  0.0 96.3 jit_solution(7928577873736781984)
XLA Ops:
  0.7 94.2 %year_sweeps.1 = f32[6,16,128]{2,1,0:T(8,128)} custom-call(s32[1,256]{1,0:T(1,128)} %cols_ref.1, s32[1,1]{1,0:T(1,128)S(6)} %copy.8.count_ref, s32[1,256]{1,0:T(1,128)} %rows_ref.1, s32[16,16]{1,0:T(8,128)} %depth_ref.1, f32[6,16,128]{2,1,0:T(8,128)} %bitcast.9, bf16[256,128,128]{2,1,0:T(8,128)(2,1)} %bitcast.7), custom_call_target="tpu_custom_call" | custom-call | tf_op jit(solution)/shard_map/year_sweeps/pallas_call | solution.py:411
  94.9 1.4 %copy.9 = f32[1,16,6,128]{3,1,2,0:T(8,128)} copy(f32[1,16,6,128]{3,1,2,0:T(8,128)} %bitcast.8) | data formatting | bytes 98304

commit v4 on v3

--- a/solution.py
+++ b/solution.py
@@ -212,12 +212,17 @@
         )
 
     def gather_rows(held, turn, half, first):
+        columns = jnp.concatenate(
+            [
+                terms[pl.ds(first + t, slots, stride=pad), :].astype(jnp.bfloat16)
+                for t in range(part)
+            ], 1,
+        )
+        sums = jnp.dot(pick[held], columns, preferred_element_type=jnp.float32)
+        sums = sums.astype(jnp.bfloat16)
         for t in range(part):
-            terms_t = terms[pl.ds(first + t, slots, stride=pad), :].astype(jnp.bfloat16)
-            rows_t = jnp.dot(pick[held], terms_t, preferred_element_type=jnp.float32)
-            rows_t = rows_t.astype(jnp.bfloat16)
             for g in range(ngroups):
-                send_v[turn, half, g, t] = rows_t[g * blk:(g + 1) * blk]
+                send_v[turn, half, g, t] = sums[g * blk:(g + 1) * blk, t * block:(t + 1) * block]
 
     def total(slot, half):
         got = [recv_v[slot, half, g].astype(jnp.float32) for g in range(ngroups)]
@@ -410,7 +415,7 @@
     smem = pl.BlockSpec(memory_space=pltpu.SMEM)
     result = pl.pallas_call(
         functools.partial(kernel, dims),
-        out_shape=jax.ShapeDtypeStruct((tracers, blk, block), jnp.float32),
+        out_shape=pltpu.VMEM((tracers, blk, block), jnp.float32),
         in_specs=[vmem, smem, vmem, vmem, vmem, pl.BlockSpec(memory_space=pltpu.HBM)],
         out_specs=vmem,
         scratch_shapes=[

time: 96.6 us -> 94.8 us (0.981)
  no operation moved by 1% of the time
where the time goes in v4:
time: 94.8 us; the launch traced here: 94.7 us
  Pallas kernels  93.4 us (99%)
    pallas_call x1, Pallas kernels, on_device(): pl.pallas_call(functools.partial(kernel, dims), out_shape=pltpu.VMEM((tra...  93.4 us

profile of v4, /device:TPU:0, one launch (start us, length us, event | category | flops | bytes accessed | tf_op | source)
XLA Modules:
  0.0 94.7 jit_solution(14309225716300679816)
XLA Ops:
  0.7 93.4 %year_sweeps.1 = f32[6,16,128]{2,1,0:T(8,128)S(1)} custom-call(s32[1,256]{1,0:T(1,128)} %cols_ref.1, s32[1,1]{1,0:T(1,128)S(6)} %copy.9.count_ref, s32[1,256]{1,0:T(1,128)} %rows_ref.1, s32[16,16]{1,0:T(8,128)} %depth_ref.1, f32[6,16,128]{2,1,0:T(8,128)} %bitcast.9, bf16[256,128,128]{2,1,0:T(8,128)(2,1)} %bitcast.8), custom_call_target="tpu_custom_call" | custom-call | tf_op jit(solution)/shard_map/year_sweeps/pallas_call | solution.py:416
  94.0 0.6 copy.8

commit v5 on v4

--- a/solution.py
+++ b/solution.py
@@ -8,7 +8,7 @@
 from jax.sharding import PartitionSpec as P
 
 MESH = pl.DeviceIdType.MESH
-CHUNKS = 8
+CHUNKS = 4
 HALVES = 2
 
 
@@ -157,31 +157,32 @@
         terms[pl.ds(s * pad, 2 * pad), :] = out
 
     def link(turn, half, g, target_month, slot):
+        if isinstance(g, int):
+            shift = deltas[g]
+        else:
+            shift = jnp.where(g == 1, ncols - 1, 1)
         return pltpu.make_async_remote_copy(
             src_ref=send_v.at[turn, half, g],
             dst_ref=recv_v.at[slot, half, g],
             send_sem=send_sem.at[turn, half, g],
             recv_sem=recv_sem.at[slot, half, g],
-            device_id={"month": target_month, "cols": lax.rem(here + deltas[g], ncols)},
+            device_id={"month": target_month, "cols": lax.rem(here + shift, ncols)},
             device_id_type=MESH,
         )
 
     other = lax.rem(month + 2, months)
-
-    def send_all(turn, half, target_month, slot, groups):
-        near_end = lax.rem(here, 4) == 3
-
-        @pl.when(near_end)
-        def _():
-            for g in (2, 3, 1, 0):
-                if g in groups:
-                    link(turn, half, g, target_month, slot).start()
-
-        @pl.when(jnp.logical_not(near_end))
-        def _():
-            for g in (1, 3, 2, 0):
-                if g in groups:
-                    link(turn, half, g, target_month, slot).start()
+    far = jnp.where(lax.rem(here, 4) == 3, 2, 1)
+
+    def send_all(turn, half, target_month, slot, own):
+        link(turn, half, far, target_month, slot).start()
+        link(turn, half, 3, target_month, slot).start()
+        link(turn, half, 3 - far, target_month, slot).start()
+        if own is True:
+            link(turn, half, 0, target_month, slot).start()
+        else:
+            @pl.when(own)
+            def _():
+                link(turn, half, 0, target_month, slot).start()
 
     def back(half):
         return pltpu.make_async_remote_copy(
@@ -252,7 +253,7 @@
             gather_rows(0, 0, half, half * part)
             if half == 0:
                 meet()
-            send_all(0, half, last - 1, 0, everyone)
+            send_all(0, half, last - 1, 0, True)
 
         for k in range(CHUNKS):
             turn_tiles(k)
@@ -292,6 +293,12 @@
         opening = (month == last) & (sweep == 0)
         spare = (month == last - 1) & (turn == 0)
         took = jnp.where(month == last, 1, 0)
+        ending = (month == 1) & (turn == 3)
+        onward = jnp.where(ending, 0, lax.rem(month + months - 2, months))
+        goes_to = jnp.where(spare, month - 1, jnp.where(held == 0, month, onward))
+        wraps = jnp.where((month == 1) & (turn == 1), 2, 0)
+        lands = jnp.where(ending, 0, 2 * sweep + wraps)
+        lands_in = jnp.where(spare, 0, jnp.where(held == 0, turn + 1, lands))
 
         @pl.when(odd & (held == 1) & (half == 0) & (sweep == took))
         def _():
@@ -325,22 +332,7 @@
             lax.fori_loop(0, slots // 2, run, 0, unroll=slots // 2)
             gather_rows(held, turn, half, 0)
 
-            @pl.when(spare)
-            def _():
-                send_all(turn, half, month - 1, 0, everyone)
-
-            @pl.when(odd & (held == 0))
-            def _():
-                send_all(turn, half, month, turn + 1, everyone[1:])
-
-            @pl.when(odd & (held == 1) & ((month > 1) | (sweep == 0)))
-            def _():
-                ahead = jnp.where(month == 1, 2, 0)
-                send_all(turn, half, lax.rem(month + months - 2, months), 2 * sweep + ahead, everyone)
-
-            @pl.when(odd & (held == 1) & (month == 1) & (sweep == 1))
-            def _():
-                send_all(turn, half, 0, 0, everyone)
+            send_all(turn, half, goes_to, lands_in, (held == 1) | spare)
 
             @pl.when((sweep == 1) & (held == 1))
             def _():

time: 94.8 us -> 94.1 us (level)
  no operation moved by 1% of the time
where the time goes in v5:
time: 94.1 us; the launch traced here: 93.9 us
  Pallas kernels  92.6 us (98%)
    pallas_call x1, Pallas kernels, on_device(): pl.pallas_call(functools.partial(kernel, dims), out_shape=pltpu.VMEM((tra...  92.6 us

profile of v5, /device:TPU:0, one launch (start us, length us, event | category | flops | bytes accessed | tf_op | source)
XLA Modules:
  0.0 93.9 jit_solution(13414284473270777042)
XLA Ops:
  0.7 92.6 %year_sweeps.1 = f32[6,16,128]{2,1,0:T(8,128)S(1)} custom-call(s32[1,256]{1,0:T(1,128)} %cols_ref.1, s32[1,1]{1,0:T(1,128)S(6)} %copy.9.count_ref, s32[1,256]{1,0:T(1,128)} %rows_ref.1, s32[16,16]{1,0:T(8,128)} %depth_ref.1, f32[6,16,128]{2,1,0:T(8,128)} %bitcast.9, bf16[256,128,128]{2,1,0:T(8,128)(2,1)} %bitcast.8), custom_call_target="tpu_custom_call" | custom-call | tf_op jit(solution)/shard_map/year_sweeps/pallas_call | solution.py:408
  93.3 0.6 copy.8

commit v6 on v5

--- a/solution.py
+++ b/solution.py
@@ -172,6 +172,7 @@
 
     other = lax.rem(month + 2, months)
     far = jnp.where(lax.rem(here, 4) == 3, 2, 1)
+    far_in = jnp.where(lax.rem(here, 4) == 0, 2, 1)
 
     def send_all(turn, half, target_month, slot, own):
         link(turn, half, far, target_month, slot).start()
@@ -320,10 +321,16 @@
             def _():
                 recv_v[turn, half, 0] = send_v[turn - held, half, 0]
 
-            for g in range(1, ngroups):
+            for g in (3, 3 - far_in):
                 link(turn, half, g, other, turn).wait_recv()
-            state = total(turn, half)
-            set_x(state + force_v[held, pl.ds(half * part, part)])
+            near = (
+                recv_v[turn, half, 0].astype(jnp.float32)
+                + recv_v[turn, half, 3 - far_in].astype(jnp.float32)
+            ) + recv_v[turn, half, 3].astype(jnp.float32)
+            push = force_v[held, pl.ds(half * part, part)]
+            link(turn, half, far_in, other, turn).wait_recv()
+            state = (near + recv_v[turn, half, far_in].astype(jnp.float32)) * wet_v[...][None]
+            set_x(state + push)
 
             def run(i, carry):
                 pair(i, held, True)

time: 94.1 us -> 93.9 us (level)
  no operation moved by 1% of the time
where the time goes in v6:
time: 93.9 us; the launch traced here: 93.7 us
  Pallas kernels  92.4 us (98%)
    pallas_call x1, Pallas kernels, on_device(): pl.pallas_call(functools.partial(kernel, dims), out_shape=pltpu.VMEM((tra...  92.4 us

profile of v6, /device:TPU:0, one launch (start us, length us, event | category | flops | bytes accessed | tf_op | source)
XLA Modules:
  0.0 93.7 jit_solution(8453374099661145926)
XLA Ops:
  0.7 92.4 %year_sweeps.1 = f32[6,16,128]{2,1,0:T(8,128)S(1)} custom-call(s32[1,256]{1,0:T(1,128)} %cols_ref.1, s32[1,1]{1,0:T(1,128)S(6)} %copy.9.count_ref, s32[1,256]{1,0:T(1,128)} %rows_ref.1, s32[16,16]{1,0:T(8,128)} %depth_ref.1, f32[6,16,128]{2,1,0:T(8,128)} %bitcast.9, bf16[256,128,128]{2,1,0:T(8,128)(2,1)} %bitcast.8), custom_call_target="tpu_custom_call" | custom-call | tf_op jit(solution)/shard_map/year_sweeps/pallas_call | solution.py:415
  93.1 0.6 copy.8

commit v7 on v6

--- a/solution.py
+++ b/solution.py
@@ -133,7 +133,7 @@
     def set_x(x):
         x = x.astype(jnp.bfloat16).astype(jnp.float32)
         for t in range(x.shape[0]):
-            x_rows[:, t, :] = x[t]
+            x_rows[0:blk, t, :] = x[t]
 
     def pair(g, held, swapped):
         s = 2 * g
@@ -419,8 +419,8 @@
         out_specs=vmem,
         scratch_shapes=[
             pltpu.VMEM((2, slots, block, block), jnp.bfloat16),
-            pltpu.VMEM((blk, pad, block), jnp.float32),
-            pltpu.VMEM((slots * pad, block), jnp.float32),
+            pltpu.VMEM((blk + 1, pad, block), jnp.float32),
+            pltpu.VMEM((slots * pad + pad, block), jnp.float32),
             pltpu.VMEM((2, 4 * blk, slots), jnp.bfloat16),
             pltpu.VMEM((2, tracers, blk, block), jnp.float32),
             pltpu.VMEM((blk, block), jnp.float32),

time: 93.9 us -> 93.9 us (level)
  no operation moved by 1% of the time
where the time goes in v7:
time: 93.9 us; the launch traced here: 93.8 us
  Pallas kernels  92.5 us (99%)
    pallas_call x1, Pallas kernels, on_device(): pl.pallas_call(functools.partial(kernel, dims), out_shape=pltpu.VMEM((tra...  92.5 us

profile of v7, /device:TPU:0, one launch (start us, length us, event | category | flops | bytes accessed | tf_op | source)
XLA Modules:
  0.0 93.8 jit_solution(16808306869127762715)
XLA Ops:
  0.7 92.5 %year_sweeps.1 = f32[6,16,128]{2,1,0:T(8,128)S(1)} custom-call(s32[1,256]{1,0:T(1,128)} %cols_ref.1, s32[1,1]{1,0:T(1,128)S(6)} %copy.9.count_ref, s32[1,256]{1,0:T(1,128)} %rows_ref.1, s32[16,16]{1,0:T(8,128)} %depth_ref.1, f32[6,16,128]{2,1,0:T(8,128)} %bitcast.9, bf16[256,128,128]{2,1,0:T(8,128)(2,1)} %bitcast.8), custom_call_target="tpu_custom_call" | custom-call | tf_op jit(solution)/shard_map/year_sweeps/pallas_call | solution.py:415
  93.1 0.6 copy.8

commit v8 on v7

--- a/solution.py
+++ b/solution.py
@@ -286,11 +286,9 @@
             turn_tiles(k)
         meet()
 
-    def step(k, carry):
-        sweep = k // (2 * HALVES)
-        held = lax.rem(k // HALVES, 2)
-        half = lax.rem(k, HALVES)
-        turn = 2 * sweep + held
+    def step(turn, half):
+        sweep = turn // 2
+        held = lax.rem(turn, 2)
         opening = (month == last) & (sweep == 0)
         spare = (month == last - 1) & (turn == 0)
         took = jnp.where(month == last, 1, 0)
@@ -350,9 +348,12 @@
                 back_v[half] = total(turn, half)
                 back(half).start()
 
+    def both(turn, carry):
+        for half in range(HALVES):
+            step(turn, half)
         return carry
 
-    lax.fori_loop(0, 4 * HALVES, step, 0)
+    lax.fori_loop(0, 4, both, 0)
 
     @pl.when(month == last - 1)
     def _():

time: 93.9 us -> 93.9 us (level)
  no operation moved by 1% of the time
where the time goes in v8:
time: 93.9 us; the launch traced here: 93.7 us
  Pallas kernels  92.4 us (98%)
    pallas_call x1, Pallas kernels, on_device(): pl.pallas_call(functools.partial(kernel, dims), out_shape=pltpu.VMEM((tra...  92.4 us

profile of v8, /device:TPU:0, one launch (start us, length us, event | category | flops | bytes accessed | tf_op | source)
XLA Modules:
  0.0 93.7 jit_solution(5671237997450629718)
XLA Ops:
  0.7 92.4 %year_sweeps.1 = f32[6,16,128]{2,1,0:T(8,128)S(1)} custom-call(s32[1,256]{1,0:T(1,128)} %cols_ref.1, s32[1,1]{1,0:T(1,128)S(6)} %copy.9.count_ref, s32[1,256]{1,0:T(1,128)} %rows_ref.1, s32[16,16]{1,0:T(8,128)} %depth_ref.1, f32[6,16,128]{2,1,0:T(8,128)} %bitcast.9, bf16[256,128,128]{2,1,0:T(8,128)(2,1)} %bitcast.8), custom_call_target="tpu_custom_call" | custom-call | tf_op jit(solution)/shard_map/year_sweeps/pallas_call | solution.py:416
  93.1 0.6 copy.8
